TPU v7x, 32 devices: a whole 2x2x4 slice. The times are simulated.
32 devices in a mesh: group: 2 (over x), dp: 16 (over z, y, core).
Axes of the slice: x: 2, y: 2, z: 4, core: 2. Of those that a mesh axis runs over, the one named last changes fastest.
Arguments:
- candidate_queries: bfloat16 [256, 8, 16, 4096], P(('group', 'dp')), parts along dimension 0, may hold values from -10 to 10
- target_states: bfloat16 [256, 32, 1024], P(('group', 'dp')), parts along dimension 0, may hold values from -4 to 4
- target_queries: bfloat16 [256, 32, 4096], P(('group', 'dp')), parts along dimension 0, may hold values from -10 to 10
- candidate_states: bfloat16 [2048, 16, 1024], P(('group', 'dp')), parts along dimension 0, may hold values from -4 to 4
- target_length: int32 [256], P(('group', 'dp')), parts along dimension 0, may hold values from 2 to 32
- candidate_length: int32 [256, 8], P(('group', 'dp')), parts along dimension 0, may hold values from 2 to 16
- candidate_row: int32 [256, 8], P(('group', 'dp')), parts along dimension 0, may hold values from 0 to 63, as said below
- direct_readout: bfloat16 [4096], replicated, may hold values from -0.5 to 0.5
- channel_readout: bfloat16 [4096], replicated, may hold values from -0.5 to 0.5
Outputs:
- rescored: float32 [2048], P(('group', 'dp')), parts along dimension 0
There are 2 independent parts, one for each index of `group`. A program takes and returns all parts, laid end to end along the dimension named above; an argument that names none is the same for every part. Nothing has to cross between parts.
Inputs may be any that keep to these rules, and one draw needn't show every extreme that they name: `candidate_row`: on the 8 targets of each aligned block (targets b * 8 to (b + 1) * 8 - 1), the 64 entries hold every value from 0 to 63 once.
All inputs are finite; a program needn't handle non-finite values.
Results may differ from a plain program's by a relative error of at most 0.0021.
Values may be sent and summed in bfloat16 or wider, within the bound.
A program may use at most 128 MiB of HBM per device.

v0:
```python
import math

import jax
import jax.numpy as jnp
from jax import lax
from jax.sharding import PartitionSpec as P

QUERY_HEADS = 32
KEY_VALUE_HEADS = 4
HEAD_SIZE = 128


masked_score = -1e30


def softmax_weights(scores, usable):
    scores = jnp.where(usable, scores, masked_score)
    highest = jnp.max(scores, axis=-1, keepdims=True)
    weights = jnp.exp(scores - highest)
    return (weights / jnp.sum(weights, axis=-1, keepdims=True)).astype(jnp.bfloat16)


def attend_shared(query_rows, hidden_states, length):
    batch_groups, count_of_rows, model_width = query_rows.shape
    length_of_keys = hidden_states.shape[1]
    grouped_heads = query_rows.reshape(
        batch_groups, count_of_rows, KEY_VALUE_HEADS, QUERY_HEADS // KEY_VALUE_HEADS, HEAD_SIZE
    )
    split_halves = hidden_states.reshape(
        batch_groups, length_of_keys, 2, KEY_VALUE_HEADS, HEAD_SIZE
    )
    scores = jnp.einsum(
        "brgqd,bkgd->bgqrk",
        grouped_heads,
        split_halves[:, :, 0],
        preferred_element_type=jnp.float32,
    ) * (1.0 / math.sqrt(HEAD_SIZE))
    usable = (jnp.arange(length_of_keys, dtype=jnp.int32)[None, :] < length[:, None])[
        :, None, None, None, :
    ]
    weights = softmax_weights(scores, usable)
    mixture = jnp.einsum(
        "bgqrk,bkgd->brgqd", weights, split_halves[:, :, 1], preferred_element_type=jnp.float32
    )
    return mixture.astype(jnp.bfloat16).reshape(batch_groups, count_of_rows, model_width)


def attend_paired(query_rows, hidden_states, length):
    batch_groups, count_of_rows, model_width = query_rows.shape
    count_of_pairs, length_of_keys = (hidden_states.shape[1], hidden_states.shape[2])
    grouped_heads = query_rows.reshape(
        batch_groups, count_of_rows, KEY_VALUE_HEADS, QUERY_HEADS // KEY_VALUE_HEADS, HEAD_SIZE
    )
    split_halves = hidden_states.reshape(
        batch_groups, count_of_pairs, length_of_keys, 2, KEY_VALUE_HEADS, HEAD_SIZE
    )
    scores = jnp.einsum(
        "brgqd,bpkgd->bpgqrk",
        grouped_heads,
        split_halves[:, :, :, 0],
        preferred_element_type=jnp.float32,
    ) * (1.0 / math.sqrt(HEAD_SIZE))
    usable = (jnp.arange(length_of_keys, dtype=jnp.int32)[None, None, :] < length[:, :, None])[
        :, :, None, None, None, :
    ]
    weights = softmax_weights(scores, usable)
    mixture = jnp.einsum(
        "bpgqrk,bpkgd->bprgqd",
        weights,
        split_halves[:, :, :, 1],
        preferred_element_type=jnp.float32,
    )
    return mixture.astype(jnp.bfloat16).reshape(
        batch_groups, count_of_pairs, count_of_rows, model_width
    )


def pooled(mixture, readout, length):
    tokens = jnp.dot(mixture, readout, preferred_element_type=jnp.float32)
    usable = jnp.arange(tokens.shape[-1], dtype=jnp.int32) < length[..., None]
    return jnp.sum(jnp.where(usable, tokens, 0.0), axis=-1) / length.astype(jnp.float32)


def on_device(
    candidate_queries,
    target_states,
    target_queries,
    candidate_states,
    target_length,
    candidate_length,
    candidate_row,
    direct_readout,
    channel_readout,
):
    target_count, slot_count, source_length, model_width = candidate_queries.shape
    candidate_count = target_count * slot_count
    direct_mix = attend_shared(
        candidate_queries.reshape(target_count, slot_count * source_length, model_width),
        target_states,
        target_length,
    )
    direct = pooled(
        direct_mix.reshape(target_count, slot_count, source_length, model_width),
        direct_readout,
        candidate_length,
    )
    flat_rows = candidate_row.reshape(candidate_count)
    matches = flat_rows[None, :] == jnp.arange(candidate_count, dtype=jnp.int32)[:, None]
    arrived = lax.all_to_all(candidate_states, "dp", split_axis=0, concat_axis=0, tiled=True)
    paired = jnp.take(arrived, flat_rows, axis=0).reshape(
        target_count, slot_count, source_length, arrived.shape[2]
    )
    channel_mix = attend_paired(target_queries, paired, candidate_length)
    target_counts = jnp.broadcast_to(target_length[:, None], candidate_length.shape)
    channel = pooled(channel_mix, channel_readout, target_counts)
    combined = (direct + channel).reshape(candidate_count)
    outgoing = jnp.sum(jnp.where(matches, combined[None, :], 0.0), axis=1)
    result = lax.all_to_all(outgoing, "dp", split_axis=0, concat_axis=0, tiled=True)
    return result


def solution(mesh):
    in_specs = (
        P(("group", "dp"), None, None, None),
        P(("group", "dp"), None, None),
        P(("group", "dp"), None, None),
        P(("group", "dp"), None, None),
        P(("group", "dp")),
        P(("group", "dp"), None),
        P(("group", "dp"), None),
        P(),
        P(),
    )
    out_specs = P(("group", "dp"))
    return jax.shard_map(
        on_device, mesh=mesh, in_specs=in_specs, out_specs=out_specs, check_vma=False
    )
```

profile of v0, /device:TPU:0, one launch (start us, length us, event | category | flops | bytes accessed | tf_op | source)
XLA Modules:
  0.0 181.3 jit_solution(12942013003783667898)
XLA Ops:
  0.0 7.6 %all-to-all-start = ((bf16[64,16,1024]{2,1,0:T(8,128)(2,1)}), bf16[64,16,1024]{2,1,0:T(8,128)(2,1)S(1)}, u32[]{:S(2)}, u32[]{:S(2)}) async-start(bf16[64,16,1024]{2,1,0:T(8,128)(2,1)} %param.12), calls=%async_computation | async-start | bytes 4194304 | tf_op jit(solution)/shard_map/all_to_all | solution.py:109
  7.6 0.1 reshape.78
  7.7 0.1 eq.15
  7.7 3.4 %copy.59 = bf16[32,8,32,128]{3,2,1,0:T(8,128)(2,1)} copy(bf16[32,8,32,128]{3,1,2,0:T(8,128)(2,1)} %bitcast.90) | data formatting | bytes 4194304
  11.2 0.4 reshape.77
  11.6 9.4 %copy.58 = bf16[128,8,32,128]{3,2,1,0:T(8,128)(2,1)} copy(bf16[128,8,32,128]{3,1,2,0:T(8,128)(2,1)} %bitcast.89) | data formatting | bytes 16777216
  21.0 0.1 iota_compare_fusion.3
  21.1 0.2 fusion.39
  21.3 6.4 %fusion.7 = f32[8,4,32,128,8]{3,2,4,1,0:T(8,128)S(1)} fusion(bf16[8,128,4,8,128]{4,3,2,1,0:T(8,128)(2,1)} %bitcast.88, bf16[8,32,1,4,128]{4,3,2,1,0:T(4,128)(2,1)S(1)} %get-tuple-element.6), kind=kOutput, calls=%fused_computation.11 | convolution fusion | flops 268435456 | bytes 12845056 | tf_op jit(solution)/shard_map/brgqd,bkgd->bgqrk/dot_general | solution.py:32
  27.7 2.2 %fusion.45 = (f32[8,4,8,128]{3,2,1,0:T(8,128)S(1)}, f32[8,4,8,128,32]{3,4,2,1,0:T(8,128)S(1)}) fusion(f32[8,4,32,128,8]{3,2,4,1,0:T(8,128)S(1)} %fusion.7, pred[8,32]{1,0:T(8,128)(4,1)S(1)} %iota_compare_fusion.3), kind=kOutput, calls=%fused_computation.60 | output fusion | flops 6291487 | bytes 8519936 | tf_op jit(solution)/shard_map/sub | solution.py:19
  30.0 4.7 %convert_bitcast_fusion.1 = bf16[8,128,4,8,128]{4,1,3,2,0:T(8,128)(2,1)} fusion(f32[8,4,8,128,32]{3,4,2,1,0:T(8,128)S(1)} %get-tuple-element.10, f32[8,4,8,128]{3,2,1,0:T(8,128)S(1)} %get-tuple-element.9, bf16[8,32,1,4,128]{4,3,2,1,0:T(4,128)(2,1)S(1)} %get-tuple-element.5), kind=kOutput, calls=%fused_computation.15 | convolution fusion | flops 274726912 | bytes 12976128 | tf_op jit(solution)/shard_map/bgqrk,bkgd->brgqd/dot_general | solution.py:42
  34.7 12.0 %copy.36 = bf16[8,128,4,8,128]{4,3,2,1,0:T(8,128)(2,1)} copy(bf16[8,128,4,8,128]{4,1,3,2,0:T(8,128)(2,1)} %convert_bitcast_fusion.1) | data formatting | bytes 16777216 | tf_op jit(solution)/shard_map/convert_element_type | solution.py:45
  46.7 13.3 %reshape_reshape.8 = bf16[8,8,16,4096]{3,2,1,0:T(8,128)(2,1)} reshape(bf16[8,128,4,8,128]{4,3,2,1,0:T(8,128)(2,1)} %copy.36) | data formatting | bytes 16777216 | tf_op jit(solution)/shard_map/reshape;reshape | solution.py:103
  60.1 13.2 %fusion.32 = f32[1,8,8,16]{3,0,2,1:T(1,128)S(1)} fusion(bf16[8,8,16,4096]{3,2,1,0:T(8,128)(2,1)} %reshape_reshape.8, bf16[4096,1,1,1]{0,1,2,3:T(2,128)(2,1)S(1)} %reshape.91), kind=kOutput, calls=%fused_computation.45 | convolution fusion | flops 8388608 | bytes 8400896 | tf_op jit(solution)/shard_map/dot_general | solution.py:79
  73.3 0.2 select_reduce_fusion.2
  73.5 0.1 iota_compare_fusion.1
  73.6 2.0 %gather_fusion = bf16[64,16,1024]{2,1,0:T(8,128)(2,1)} fusion(bf16[64,16,1024]{2,1,0:T(8,128)(2,1)S(1)} %all-to-all-done, s32[1024]{0:T(1024)S(1)} %pad_clamp_fusion), kind=kCustom, calls=%fused_computation | custom fusion | bytes 4194560 | tf_op jit(solution)/shard_map/jit(_take)/gather | solution.py:110
  75.6 3.2 %gather.7 = bf16[8,8,16,2,4,128]{5,4,3,2,1,0:T(4,128)(2,1)S(1)} reshape(bf16[64,16,1024]{2,1,0:T(8,128)(2,1)} %gather_fusion) | data formatting | bytes 4194304 | tf_op jit(solution)/shard_map/jit(_take)/gather | solution.py:110
  78.8 1.6 copy_select_fusion
  80.5 15.7 %fusion.40 = (f32[8,8,4,8,32]{4,3,1,2,0:T(8,128)}, f32[8,8,4,8,32,16]{4,5,3,1,2,0:T(8,128)}) fusion(pred[8,8,16]{2,1,0:T(8,128)(4,1)S(1)} %iota_compare_fusion.1, bf16[8,32,4,8,128,1]{4,3,2,1,0,5:T(8,128)(2,1)} %bitcast.91, bf16[8,8,16,2,4,128]{5,2,1,4,0,3:T(8,128)(2,1)} %copy_select_fusion), kind=kOutput, calls=%fused_computation.59 | convolution fusion | flops 272629760 | bytes 7603200 | tf_op jit(solution)/shard_map/sub | solution.py:19
  96.1 13.3 %convert_bitcast_fusion = bf16[8,8,32,4,8,128]{5,2,4,3,1,0:T(8,128)(2,1)} fusion(f32[8,8,4,8,32,16]{4,5,3,1,2,0:T(8,128)} %get-tuple-element.8, f32[8,8,4,8,32]{4,3,1,2,0:T(8,128)} %get-tuple-element.7, bf16[8,8,16,2,4,128]{5,2,1,4,0,3:T(8,128)(2,1)S(1)} %copy-done), kind=kOutput, calls=%fused_computation.7 | convolution fusion | flops 278921216 | bytes 22282240 | tf_op jit(solution)/shard_map/bpgqrk,bpkgd->bprgqd/dot_general | solution.py:67
  109.5 17.5 %copy.41 = bf16[8,8,32,4,8,128]{5,4,3,2,1,0:T(8,128)(2,1)} copy(bf16[8,8,32,4,8,128]{5,2,4,3,1,0:T(8,128)(2,1)} %convert_bitcast_fusion) | data formatting | bytes 33554432 | tf_op jit(solution)/shard_map/convert_element_type | solution.py:73
  127.0 25.3 %reshape.80 = bf16[8,8,32,4096]{3,2,1,0:T(8,128)(2,1)} reshape(bf16[8,8,32,4,8,128]{5,4,3,2,1,0:T(8,128)(2,1)} %copy.41) | data formatting | bytes 33554432 | tf_op jit(solution)/shard_map/reshape | solution.py:73
  152.3 14.4 %fusion.30 = f32[1,8,8,32]{3,0,2,1:T(1,128)S(1)} fusion(bf16[8,8,32,4096]{3,2,1,0:T(8,128)(2,1)} %reshape.80, bf16[4096,1,1,1]{0,1,2,3:T(2,128)(2,1)S(1)} %reshape.96), kind=kOutput, calls=%fused_computation.43 | convolution fusion | flops 16777216 | bytes 16793600 | tf_op jit(solution)/shard_map/dot_general | solution.py:79
  166.7 0.2 select_reduce_fusion.1
  167.0 0.1 broadcast_in_dim.85
  167.0 0.1 select_reduce_fusion
  167.2 0.1 all_to_all.12
  167.3 12.3 %all_to_all.17 = f32[16,4,1]{1,2,0:T(1,128)S(1)} all-to-all(f32[16,4,1]{1,2,0:T(1,128)S(1)} %bitcast.94), channel_id=1, replica_groups=mesh['group'=2,'dp'=16] {'dp'}, dimensions={0} | all-to-all | bytes 512 | tf_op jit(solution)/shard_map/all_to_all | solution.py:118
  179.5 0.5 broadcast.70
  180.0 0.7 reduce.3
  180.7 0.6 all_to_all.14
  (22 shorter events, 0.2 us)
Async XLA Ops:
  0.0 7.6 %copy-start.2 = (s32[8,8]{1,0:T(8,128)S(1)}, s32[8,8]{1,0:T(8,128)}, u32[]{:S(2)}) copy-start(s32[8,8]{1,0:T(8,128)} %param.15) | copy-start | bytes 772
  0.0 11.2 %copy-start.4 = (bf16[4096]{0:T(1024)(128)(2,1)S(1)}, bf16[4096]{0:T(1024)(128)(2,1)}, u32[]{:S(2)}) copy-start(bf16[4096]{0:T(1024)(128)(2,1)} %param.17) | copy-start | bytes 24580
  0.0 11.2 %copy-start.1 = (bf16[8,32,1024]{2,1,0:T(8,128)(2,1)S(1)}, bf16[8,32,1024]{2,1,0:T(8,128)(2,1)}, u32[]{:S(2)}) copy-start(bf16[8,32,1024]{2,1,0:T(8,128)(2,1)} %param.10) | copy-start | bytes 1572868
  0.0 73.6 %all-to-all-start = ((bf16[64,16,1024]{2,1,0:T(8,128)(2,1)}), bf16[64,16,1024]{2,1,0:T(8,128)(2,1)S(1)}, u32[]{:S(2)}, u32[]{:S(2)}) async-start(bf16[64,16,1024]{2,1,0:T(8,128)(2,1)} %param.12), calls=%async_computation | async-start | bytes 4194304 | tf_op jit(solution)/shard_map/all_to_all | solution.py:109
  11.6 9.5 %copy-start.6 = (s32[8]{0:T(128)S(1)}, s32[8]{0:T(128)}, u32[]{:S(2)}) copy-start(s32[8]{0:T(128)} %param.13) | copy-start | bytes 100
  46.7 13.3 %copy-start.5 = (bf16[4096]{0:T(1024)(128)(2,1)S(1)}, bf16[4096]{0:T(1024)(128)(2,1)}, u32[]{:S(2)}) copy-start(bf16[4096]{0:T(1024)(128)(2,1)} %param.16) | copy-start | bytes 24580
  60.1 13.2 %copy-start.3 = (s32[8,8]{1,0:T(8,128)S(1)}, s32[8,8]{1,0:T(8,128)}, u32[]{:S(2)}) copy-start(s32[8,8]{1,0:T(8,128)} %param.14) | copy-start | bytes 772
  80.5 15.7 %copy-start = (bf16[8,8,16,2,4,128]{5,2,1,4,0,3:T(8,128)(2,1)S(1)}, bf16[8,8,16,2,4,128]{5,2,1,4,0,3:T(8,128)(2,1)}, u32[]{:S(2)}) copy-start(bf16[8,8,16,2,4,128]{5,2,1,4,0,3:T(8,128)(2,1)} %copy_select_fusion) | copy-start | bytes 6291460
where the time goes:
time: 183 us; the launch traced here: 181 us
  local copies, waits for them, and re-layouts  88.3 us (48%)
  matrix products  67.8 us (37%)
  blocking collectives  12.3 us (7%)
  starting transfers between devices  7.56 us (4%)
  other arithmetic  5.21 us (3%)
    dot_general x2, matrix products, pooled(): tokens = jnp.dot(mixture, readout, preferred_element_type=jnp.float32)  27.6 us
    reshape x1, local copies, waits for them, and re-layouts, attend_paired(): mixture.astype(jnp.bfloat16)  25.3 us
    convert_element_type x1, local copies, waits for them, and re-layouts, attend_paired(): mixture.astype(jnp.bfloat16)  17.5 us
    sub x1, matrix products, softmax_weights(): weights = jnp.exp(scores - highest)  15.7 us
    dot_general x1, matrix products, attend_paired(): jnp.einsum('bpgqrk,bpkgd->bprgqd', weights, split_halves[:, :, :, 1], pre...  13.3 us
    another operation x1, local copies, waits for them, and re-layouts, on_device(): direct_mix.reshape(target_count, slot_count, source_length, model_width)  13.3 us
    unnamed x18, local copies, waits for them, and re-layouts  12.9 us
    all_to_all x1, blocking collectives, on_device(): lax.all_to_all(outgoing, 'dp', split_axis=0, concat_axis=0, tiled=True)  12.3 us
  transfers between devices with their start and end apart: 1, of which 0 were waited for; matrix products, arithmetic and copies ran while one was open for 36% of the time, Pallas kernels for 0%

commit v1 on v0

v1 whole, which is shorter than its diff:
```python
import functools
import math

import jax
import jax.numpy as jnp
from jax import lax
from jax.experimental import pallas as pl
from jax.experimental.pallas import tpu as pltpu
from jax.sharding import PartitionSpec as P

HEAD_SIZE = 128
AXIS = "dp"
MESH = pl.DeviceIdType.MESH
EARLY = 6
masked_score = -1e30


def dot_nt(a, b):
    return lax.dot_general(
        a, b, (((1,), (1,)), ((), ())), preferred_element_type=jnp.float32
    )


def exchange(a, b, n):
    if n & (n - 1):
        return lax.rem(a + b, n)
    out, bit = 0, 1
    while bit < n:
        out = out + lax.rem(a // bit + b // bit, 2) * bit
        bit *= 2
    return out


def expect(a, b, n):
    if n & (n - 1):
        return lax.rem(a + n - b, n)
    return exchange(a, b, n)


def ratio(scores, values, keys_left):
    keys = lax.broadcasted_iota(jnp.int32, scores.shape, 0)
    scores = jnp.where(keys < keys_left, scores, masked_score)
    highest = jnp.max(scores, axis=0, keepdims=True)
    factor = math.log2(math.e) / math.sqrt(HEAD_SIZE)
    weights = jnp.exp2((scores - highest) * factor)
    return jnp.sum(weights * values, axis=0, keepdims=True) / jnp.sum(
        weights, axis=0, keepdims=True
    )


def kernel(
    n, dims,
    table, lengths, spread, readouts, cq, ts, tq, cs,
    out,
    cq_buf, ts_buf, tq_buf, v_buf, k_buf, u_out, u_buf, ud, rd, sel, dsum, r_out, r_buf,
    in_sem, cq_sem, ks, kr, us, ur, rs, rr,
):
    T, S, I, J, H, G = dims
    C = T * S
    rpp = C // n
    hg = H // G
    D = HEAD_SIZE
    me = lax.axis_index(AXIS)

    loads = [
        pltpu.make_async_copy(cs.at[:, :, :, pl.ds(G * D, G * D)], v_buf, in_sem.at[0]),
        pltpu.make_async_copy(
            cs.at[me, :, :, pl.ds(0, G * D)], k_buf.at[me], in_sem.at[1]
        ),
        pltpu.make_async_copy(ts, ts_buf, in_sem.at[2]),
        pltpu.make_async_copy(tq, tq_buf, in_sem.at[3]),
    ]
    loads[0].start()
    loads[2].start()

    def cq_copy(t):
        return pltpu.make_async_copy(cq.at[t], cq_buf.at[t], cq_sem.at[t])

    barrier = pltpu.get_barrier_semaphore()

    def greet(k, carry):
        pl.semaphore_signal(
            barrier, inc=1, device_id={AXIS: exchange(me, k, n)}, device_id_type=MESH
        )
        return carry

    lax.fori_loop(1, n, greet, 0)
    cq_copy(0).start()

    def k_copy(p, slot):
        return pltpu.make_async_remote_copy(
            src_ref=cs.at[p, :, :, pl.ds(0, G * D)],
            dst_ref=k_buf.at[slot], send_sem=ks.at[p], recv_sem=kr.at[slot],
            device_id={AXIS: p}, device_id_type=MESH,
        )

    def u_copy(p, slot):
        return pltpu.make_async_remote_copy(
            src_ref=u_out.at[p], dst_ref=u_buf.at[slot], send_sem=us.at[p],
            recv_sem=ur.at[slot], device_id={AXIS: p}, device_id_type=MESH,
        )

    def r_copy(p, slot):
        return pltpu.make_async_remote_copy(
            src_ref=r_out.at[p], dst_ref=r_buf.at[slot], send_sem=rs.at[p],
            recv_sem=rr.at[slot], device_id={AXIS: p}, device_id_type=MESH,
        )

    def k_send(i, carry):
        p = exchange(me, n - 1 - i, n)
        k_copy(p, me).start()
        return carry

    pl.semaphore_wait(barrier, n - 1)
    early = min(EARLY, n - 1)
    lax.fori_loop(0, early, k_send, 0)
    loads[1].start()
    for t in range(1, T):
        cq_copy(t).start()
    loads[3].start()

    wide = u_out.shape[2]
    channel_r = jnp.concatenate([readouts[1]] * (wide // H), axis=0)
    row_id = lax.broadcasted_iota(jnp.int32, (wide, D), 0)
    loads[0].wait()
    u = None
    for r in range(rpp):
        for g in range(G):
            weights = jnp.where(
                row_id // hg == r * G + g, channel_r, jnp.zeros_like(channel_r)
            )
            values = v_buf[:, r, :, g * D : (g + 1) * D]
            values = values.reshape(n * I, D)
            part = dot_nt(values, weights)
            u = part if u is None else u + part
    u_out[...] = u.astype(jnp.bfloat16).reshape(n, I, wide)

    lane = lax.broadcasted_iota(jnp.int32, (wide, hg * J), 1)
    head = lax.broadcasted_iota(jnp.int32, (wide, hg * J), 0)
    for r in range(rpp):
        for g in range(G):
            hit = head == lane // J + (r * H + g * hg)
            sel[r * G + g] = jnp.where(hit, 1.0, 0.0).astype(jnp.bfloat16)

    loads[2].wait()
    rows = S * I
    for g in range(G):
        states = ts_buf[:, :, (G + g) * D : (G + g + 1) * D].reshape(T * J, D)
        for q in range(hg):
            h = g * hg + q
            rd[q * rows : (q + 1) * rows, :] = jnp.broadcast_to(
                readouts[0, h : h + 1, :], (rows, D)
            )
        ud[g] = dot_nt(states, rd[...])

    def u_send(i, carry):
        u_copy(exchange(me, n - 1 - i, n), me).start()
        return carry

    lax.fori_loop(0, n - 1, u_send, 0)
    lax.fori_loop(early, n - 1, k_send, 0)

    token = lax.rem(lax.broadcasted_iota(jnp.int32, (1, rows), 1), I)

    def direct(t, carry):
        cq_copy(t).wait()
        total = jnp.zeros((1, hg * rows), jnp.float32)
        for g in range(G):
            queries = jnp.concatenate(
                [
                    cq_buf[t, :, (g * hg + q) * D : (g * hg + q + 1) * D]
                    for q in range(hg)
                ],
                axis=0,
            )
            scores = dot_nt(ts_buf[t, :, g * D : (g + 1) * D], queries)
            values = ud[g, pl.ds(pl.multiple_of(t * J, J), J), :]
            total = total + ratio(scores, values, lengths[t])
        tokens = total[:, 0:rows]
        for q in range(1, hg):
            tokens = tokens + total[:, q * rows : (q + 1) * rows]
        count = spread[1, t]
        dsum[t] = jnp.where(token < count, tokens, 0.0) / count.astype(jnp.float32)
        return carry

    lax.fori_loop(0, T, direct, 0)

    loads[3].wait()
    lanes = out.shape[1]
    place = lax.broadcasted_iota(jnp.int32, (1, lanes), 1)
    position = lax.rem(lax.broadcasted_iota(jnp.int32, (1, hg * J), 1), J)
    direct_sums = dsum[...]
    owners = spread[0]

    def block(p):
        result = jnp.zeros((1, lanes), jnp.float32)
        sent = u_buf[p]
        for r in range(rpp):
            v = p * rpp + r
            t, source_count, target_count = table[0, v], table[1, v], table[2, v]
            total = jnp.zeros((1, hg * J), jnp.float32)
            for g in range(G):
                queries = jnp.concatenate(
                    [
                        tq_buf[t, :, (g * hg + q) * D : (g * hg + q + 1) * D]
                        for q in range(hg)
                    ],
                    axis=0,
                )
                scores = dot_nt(k_buf[p, r, :, g * D : (g + 1) * D], queries)
                values = jnp.dot(
                    sent, sel[r * G + g], preferred_element_type=jnp.float32
                )
                total = total + ratio(scores, values, source_count)
            kept = jnp.where(position < target_count, total, 0.0)
            channel = jnp.sum(kept, axis=1, keepdims=True)
            channel = channel / target_count.astype(jnp.float32)
            own = jnp.where(owners == v, direct_sums, 0.0)
            own = jnp.sum(jnp.sum(own, axis=0), axis=1, keepdims=True)
            result = result + jnp.where(place == me * rpp + r, own + channel, 0.0)
        return jnp.broadcast_to(result, (8, lanes))

    u_buf[me] = u_out[me]
    loads[1].wait()
    r_buf[me] = block(me)

    def channel_step(i, carry):
        p = expect(me, n - 1 - i, n)
        k_copy(p, p).wait_recv()
        u_copy(p, p).wait_recv()
        r_out[p] = block(p)
        r_copy(p, me).start()
        return carry

    lax.fori_loop(0, n - 1, channel_step, 0)

    def finish(i, carry):
        p = expect(me, n - 1 - i, n)
        r_copy(p, p).wait_recv()
        k_copy(p, p).wait_send()
        u_copy(p, p).wait_send()
        r_copy(p, p).wait_send()
        return carry

    lax.fori_loop(0, n - 1, finish, 0)
    out[...] = jnp.sum(r_buf[...], axis=0)


def on_device(
    n,
    candidate_queries,
    target_states,
    target_queries,
    candidate_states,
    target_length,
    candidate_length,
    candidate_row,
    direct_readout,
    channel_readout,
):
    T, S, I, QW = candidate_queries.shape
    J = target_states.shape[1]
    H = QW // HEAD_SIZE
    G = target_states.shape[2] // (2 * HEAD_SIZE)
    C = T * S
    rpp = C // n
    hg = H // G
    flat = candidate_row.reshape(C)
    each = jnp.stack(
        [
            jnp.arange(C, dtype=jnp.int32) // S,
            candidate_length.reshape(C),
            jnp.broadcast_to(target_length[:, None], (T, S)).reshape(C),
        ]
    )
    matches = flat[None, :] == jnp.arange(C, dtype=jnp.int32)[:, None]
    table = jnp.sum(jnp.where(matches[None], each[:, None, :], 0), axis=2)
    spread = jnp.broadcast_to(
        jnp.stack([candidate_row, candidate_length])[..., None], (2, T, S, I)
    ).reshape(2, T, 1, S * I)
    readouts = jnp.stack([direct_readout, channel_readout]).reshape(2, H, HEAD_SIZE)
    wide = max(128, rpp * H)
    lanes = -(-C // 128) * 128
    bf, f32 = jnp.bfloat16, jnp.float32
    vmem, smem = pltpu.VMEM, pltpu.SMEM
    anywhere = pl.BlockSpec(memory_space=pl.ANY)
    dma = pltpu.SemaphoreType.DMA
    found = pl.pallas_call(
        functools.partial(kernel, n, (T, S, I, J, H, G)),
        out_shape=jax.ShapeDtypeStruct((8, lanes), f32),
        in_specs=[
            pl.BlockSpec(memory_space=smem),
            pl.BlockSpec(memory_space=smem),
            pl.BlockSpec(memory_space=vmem),
            pl.BlockSpec(memory_space=vmem),
            anywhere, anywhere, anywhere, anywhere,
        ],
        out_specs=pl.BlockSpec(memory_space=vmem),
        scratch_shapes=[
            vmem((T, S * I, QW), bf),
            vmem(target_states.shape, bf),
            vmem(target_queries.shape, bf),
            vmem((n, rpp, I, G * HEAD_SIZE), bf),
            vmem((n, rpp, I, G * HEAD_SIZE), bf),
            vmem((n, I, wide), bf),
            vmem((n, I, wide), bf),
            vmem((G, T * J, hg * S * I), f32),
            vmem((hg * S * I, HEAD_SIZE), bf),
            vmem((rpp * G, wide, hg * J), bf),
            vmem((T, 1, S * I), f32),
            vmem((n, 8, lanes), f32),
            vmem((n, 8, lanes), f32),
            dma((4,)), dma((T,)),
            dma((n,)), dma((n,)), dma((n,)), dma((n,)), dma((n,)), dma((n,)),
        ],
        compiler_params=pltpu.CompilerParams(
            collective_id=0, has_side_effects=True, vmem_limit_bytes=60 << 20
        ),
    )(
        table, target_length, spread, readouts,
        candidate_queries.reshape(T, S * I, QW),
        target_states, target_queries,
        candidate_states.reshape(n, rpp, I, 2 * G * HEAD_SIZE),
    )
    return found[0, :C]


def solution(mesh):
    in_specs = (
        P(("group", "dp"), None, None, None),
        P(("group", "dp"), None, None),
        P(("group", "dp"), None, None),
        P(("group", "dp"), None, None),
        P(("group", "dp")),
        P(("group", "dp"), None),
        P(("group", "dp"), None),
        P(),
        P(),
    )
    return jax.shard_map(
        functools.partial(on_device, mesh.shape[AXIS]),
        mesh=mesh, in_specs=in_specs, out_specs=P(("group", "dp")), check_vma=False,
    )
```

time: 183 us -> 49.2 us (0.27)
  local copies, waits for them, and re-layouts: 88.3 us -> 4.29 us
  matrix products: 67.8 us -> 0 us
  Pallas kernels: 0 us -> 41.6 us
  blocking collectives: 12.3 us -> 0 us
  starting transfers between devices: 7.56 us -> 0 us
  other arithmetic: 5.21 us -> 2.78 us
    dot_general x5 -> x0, matrix products: 52.1 us -> none  [the longest x2 27.6 us: pooled(): tokens = jnp.dot(mixture, readout, preferred_element_type=jnp.float32)]
    pallas_call x0 -> x1, Pallas kernels: none -> 41.6 us  [on_device(): pl.pallas_call(functools.partial(kernel, n, (T, S, I, J, H, G)), out_shap...]
    convert_element_type x2 -> x0, local copies, waits for them, and re-layouts: 29.6 us -> none  [the longest x1 17.5 us: attend_paired(): mixture.astype(jnp.bfloat16)]
    reshape x3 -> x1, local copies, waits for them, and re-layouts: 25.8 us -> 0.69 us  [on_device(): spread = jnp.broadcast_to(jnp.stack([candidate_row, candidate_length])[.....]
    sub x1 -> x0, matrix products: 15.7 us -> none  [softmax_weights(): weights = jnp.exp(scores - highest)]
    unnamed x18 -> x0, local copies, waits for them, and re-layouts: 12.9 us -> none
    another operation x1 -> x2, local copies, waits for them, and re-layouts: 13.3 us -> 0.85 us  [on_device(): jnp.stack([jnp.arange(C, dtype=jnp.int32) // S, candidate_length.reshape(...]
    all_to_all x1 -> x0, blocking collectives: 12.3 us -> none  [on_device(): lax.all_to_all(outgoing, 'dp', split_axis=0, concat_axis=0, tiled=True)]
  transfers between devices with their start and end apart: 1 -> 0, of which waited for: 0 -> 0; matrix products, arithmetic and copies ran while one was open for 36% -> 0% of each run, Pallas kernels for 0% -> 0%
where the time goes in v1:
time: 49.2 us; the launch traced here: 48.7 us
  Pallas kernels  41.6 us (85%)
  local copies, waits for them, and re-layouts  4.29 us (9%)
  other arithmetic  2.78 us (6%)
    pallas_call x1, Pallas kernels, on_device(): pl.pallas_call(functools.partial(kernel, n, (T, S, I, J, H, G)), out_shap...  41.6 us
    another operation x1, other arithmetic, on_device(): jnp.stack([direct_readout, channel_readout]).reshape(2, H, HEAD_SIZE)  1.31 us
    squeeze x1, local copies, waits for them, and re-layouts, on_device(): return found[0, :C]  1.18 us

profile of v1, /device:TPU:0, one launch (start us, length us, event | category | flops | bytes accessed | tf_op | source)
XLA Modules:
  0.0 48.7 jit_solution(11403786915667701616)
XLA Ops:
  0.0 0.7 %pad_add_fusion = s32[2,8,8]{2,1,0:T(8,128)S(1)} fusion(s32[1,8,8]{2,1,0:T(8,128)} %bitcast.13, s32[1,8,8]{2,1,0:T(8,128)} %bitcast.12), kind=kLoop, calls=%fused_computation.3 | loop fusion | flops 128 | bytes 1024 | tf_op jit(solution)/shard_map/stack | solution.py:279
  0.7 0.1 broadcast_in_dim.39
  0.8 0.7 %reshape.75.spread = s32[2,8,1,128]{3,2,1,0:T(1,128)} reshape(s32[2,8,8,16]{3,2,1,0:T(8,128)S(1)} %broadcast_in_dim.39) | data formatting | bytes 16384 | tf_op jit(solution)/shard_map/reshape | solution.py:280
  1.5 0.8 %eq.19 = s32[64]{0:T(128)S(1)} reshape(s32[8,8]{1,0:T(8,128)} %param.15) | data formatting | bytes 512 | tf_op jit(solution)/shard_map/eq | solution.py:276
  2.3 0.7 %broadcast_in_dim.36 = s32[8,8]{1,0:T(8,128)S(1)} broadcast(s32[8]{0:T(128)} %lengths.1), dimensions={0} | broadcast | bytes 288 | tf_op jit(solution)/shard_map/broadcast_in_dim | solution.py:273
  3.0 0.1 stack_reshape.7
  3.1 0.8 %stack_reshape.6 = s32[1,64]{1,0:T(1,128)S(1)} reshape(s32[8,8]{1,0:T(8,128)} %param.14) | data formatting | bytes 512 | tf_op jit(solution)/shard_map/stack;reshape | solution.py:269
  3.9 0.7 %select_reduce_fusion.table = s32[3,64]{1,0:T(4,128)} fusion(s32[3,64]{1,0:T(4,128)S(1)} %pad_add_fusion.1, pred[64,64]{1,0:T(8,128)(4,1)S(1)} %iota_compare_fusion), kind=kLoop, calls=%fused_computation | loop fusion | flops 24384 | bytes 5632 | tf_op jit(solution)/shard_map/reduce_sum | solution.py:277
  4.6 1.3 %pad_maximum_fusion.readouts = bf16[2,32,128]{2,1,0:T(8,128)(2,1)} fusion(bf16[1,32,128]{2,1,0:T(8,128)(2,1)} %bitcast.14, bf16[1,32,128]{2,1,0:T(8,128)(2,1)} %bitcast.15), kind=kLoop, calls=%fused_computation.2 | loop fusion | flops 8192 | bytes 32768 | tf_op jit(solution)/shard_map/stack | solution.py:281
  5.9 41.6 %shard_map.91 = f32[8,128]{1,0:T(8,128)} custom-call(s32[3,64]{1,0:T(4,128)} %select_reduce_fusion.table, s32[8]{0:T(128)} %lengths.1, s32[2,8,1,128]{3,2,1,0:T(1,128)} %reshape.75.spread, bf16[2,32,128]{2,1,0:T(8,128)(2,1)} %pad_maximum_fusion.readouts, bf16[8,128,4096]{2,1,0:T(8,128)(2,1)} %bitcast.10, bf16[8,32,1024]{2,1,0:T(8,128)(2,1)} %ts.1, ...), custom_call_target="tpu_custom_call" | custom-call | tf_op jit(solution)/shard_map/pallas_call | solution.py:288
  47.5 1.2 %slice_bitcast_fusion = f32[64]{0:T(128)} fusion(f32[8,128]{1,0:T(8,128)} %shard_map.91), kind=kLoop, calls=%fused_computation.9 | loop fusion | bytes 512 | tf_op jit(solution)/shard_map/squeeze | solution.py:325
  (3 shorter events, 0.0 us)

commit v2 on v1

--- a/solution.py
+++ b/solution.py
@@ -11,7 +11,7 @@
 HEAD_SIZE = 128
 AXIS = "dp"
 MESH = pl.DeviceIdType.MESH
-EARLY = 6
+EARLY = 3
 masked_score = -1e30
 
 
@@ -31,6 +31,12 @@
     return out
 
 
+def turn(i, n):
+    return lax.select(
+        lax.rem(i, 2) == 0, n - 1 - i // 2, lax.max(n // 2 - 1 - i // 2, 1)
+    ) if n % 2 == 0 and n > 2 else n - 1 - i
+
+
 def expect(a, b, n):
     if n & (n - 1):
         return lax.rem(a + n - b, n)
@@ -50,9 +56,9 @@
 
 def kernel(
     n, dims,
-    table, lengths, spread, readouts, cq, ts, tq, cs,
+    stored, sources, lengths, direct_r, channel_r, cq, ts, tq, cs,
     out,
-    cq_buf, ts_buf, tq_buf, v_buf, k_buf, u_out, u_buf, ud, rd, sel, dsum, r_out, r_buf,
+    cq_buf, ts_buf, tq_buf, v_buf, k_buf, u_out, u_buf, spread, ud, rd, sel, dsum, r_out, r_buf,
     in_sem, cq_sem, ks, kr, us, ur, rs, rr,
 ):
     T, S, I, J, H, G = dims
@@ -107,7 +113,7 @@
         )
 
     def k_send(i, carry):
-        p = exchange(me, n - 1 - i, n)
+        p = exchange(me, turn(i, n), n)
         k_copy(p, me).start()
         return carry
 
@@ -120,20 +126,25 @@
     loads[3].start()
 
     wide = u_out.shape[2]
-    channel_r = jnp.concatenate([readouts[1]] * (wide // H), axis=0)
+    head_id = lax.broadcasted_iota(jnp.int32, (H, D), 0)
+    rows_r = jnp.zeros((H, D), jnp.float32)
+    for h in range(H):
+        row = channel_r[:, h * D : (h + 1) * D].astype(jnp.float32)
+        rows_r = jnp.where(head_id == h, row, rows_r)
+    rows_r = jnp.concatenate([rows_r.astype(jnp.bfloat16)] * (wide // H), axis=0)
     row_id = lax.broadcasted_iota(jnp.int32, (wide, D), 0)
     loads[0].wait()
     u = None
     for r in range(rpp):
         for g in range(G):
             weights = jnp.where(
-                row_id // hg == r * G + g, channel_r, jnp.zeros_like(channel_r)
+                row_id // hg == r * G + g, rows_r, jnp.zeros_like(rows_r)
             )
             values = v_buf[:, r, :, g * D : (g + 1) * D]
             values = values.reshape(n * I, D)
             part = dot_nt(values, weights)
             u = part if u is None else u + part
-    u_out[...] = u.astype(jnp.bfloat16).reshape(n, I, wide)
+    u_out[...] = u.reshape(n, I, wide)
 
     lane = lax.broadcasted_iota(jnp.int32, (wide, hg * J), 1)
     head = lax.broadcasted_iota(jnp.int32, (wide, hg * J), 0)
@@ -142,23 +153,34 @@
             hit = head == lane // J + (r * H + g * hg)
             sel[r * G + g] = jnp.where(hit, 1.0, 0.0).astype(jnp.bfloat16)
 
+    def u_send(i, carry):
+        u_copy(exchange(me, turn(i, n), n), me).start()
+        return carry
+
+    lax.fori_loop(0, n - 1, u_send, 0)
+    lax.fori_loop(early, n - 1, k_send, 0)
+
+    rows = S * I
+    slot = lax.broadcasted_iota(jnp.int32, (1, rows), 1) // I
+    for t in range(T):
+        held = jnp.zeros((1, rows), jnp.int32)
+        count = jnp.zeros((1, rows), jnp.int32)
+        for c in range(S):
+            held = jnp.where(slot == c, stored[t, c], held)
+            count = jnp.where(slot == c, sources[t, c], count)
+        spread[0, t] = held
+        spread[1, t] = count
+        spread[2, t] = (count * (J + 1) + lengths[t]) * T + t
+
     loads[2].wait()
-    rows = S * I
     for g in range(G):
         states = ts_buf[:, :, (G + g) * D : (G + g + 1) * D].reshape(T * J, D)
         for q in range(hg):
             h = g * hg + q
             rd[q * rows : (q + 1) * rows, :] = jnp.broadcast_to(
-                readouts[0, h : h + 1, :], (rows, D)
-            )
+                direct_r[:, h * D : (h + 1) * D].astype(jnp.float32), (rows, D)
+            ).astype(jnp.bfloat16)
         ud[g] = dot_nt(states, rd[...])
-
-    def u_send(i, carry):
-        u_copy(exchange(me, n - 1 - i, n), me).start()
-        return carry
-
-    lax.fori_loop(0, n - 1, u_send, 0)
-    lax.fori_loop(early, n - 1, k_send, 0)
 
     token = lax.rem(lax.broadcasted_iota(jnp.int32, (1, rows), 1), I)
 
@@ -191,13 +213,24 @@
     position = lax.rem(lax.broadcasted_iota(jnp.int32, (1, hg * J), 1), J)
     direct_sums = dsum[...]
     owners = spread[0]
-
-    def block(p):
+    codes = spread[2]
+
+    def lookup(p):
+        return [
+            jnp.max(jnp.where(owners == p * rpp + r, codes, 0)) for r in range(rpp)
+        ]
+
+    def block(p, found):
         result = jnp.zeros((1, lanes), jnp.float32)
-        sent = u_buf[p]
+        whole = u_buf[p]
+        high = whole.astype(jnp.bfloat16)
+        low = (whole - high.astype(jnp.float32)).astype(jnp.bfloat16)
+        sent = jnp.concatenate([high, low], axis=0)
         for r in range(rpp):
             v = p * rpp + r
-            t, source_count, target_count = table[0, v], table[1, v], table[2, v]
+            t = lax.rem(found[r], T)
+            target_count = lax.rem(found[r] // T, J + 1)
+            source_count = found[r] // (T * (J + 1))
             total = jnp.zeros((1, hg * J), jnp.float32)
             for g in range(G):
                 queries = jnp.concatenate(
@@ -211,6 +244,7 @@
                 values = jnp.dot(
                     sent, sel[r * G + g], preferred_element_type=jnp.float32
                 )
+                values = values[:I] + values[I:]
                 total = total + ratio(scores, values, source_count)
             kept = jnp.where(position < target_count, total, 0.0)
             channel = jnp.sum(kept, axis=1, keepdims=True)
@@ -222,20 +256,21 @@
 
     u_buf[me] = u_out[me]
     loads[1].wait()
-    r_buf[me] = block(me)
+    r_buf[me] = block(me, lookup(me))
 
     def channel_step(i, carry):
-        p = expect(me, n - 1 - i, n)
+        p = expect(me, turn(i, n), n)
+        found = lookup(p)
         k_copy(p, p).wait_recv()
         u_copy(p, p).wait_recv()
-        r_out[p] = block(p)
+        r_out[p] = block(p, found)
         r_copy(p, me).start()
         return carry
 
     lax.fori_loop(0, n - 1, channel_step, 0)
 
     def finish(i, carry):
-        p = expect(me, n - 1 - i, n)
+        p = expect(me, turn(i, n), n)
         r_copy(p, p).wait_recv()
         k_copy(p, p).wait_send()
         u_copy(p, p).wait_send()
@@ -265,20 +300,6 @@
     C = T * S
     rpp = C // n
     hg = H // G
-    flat = candidate_row.reshape(C)
-    each = jnp.stack(
-        [
-            jnp.arange(C, dtype=jnp.int32) // S,
-            candidate_length.reshape(C),
-            jnp.broadcast_to(target_length[:, None], (T, S)).reshape(C),
-        ]
-    )
-    matches = flat[None, :] == jnp.arange(C, dtype=jnp.int32)[:, None]
-    table = jnp.sum(jnp.where(matches[None], each[:, None, :], 0), axis=2)
-    spread = jnp.broadcast_to(
-        jnp.stack([candidate_row, candidate_length])[..., None], (2, T, S, I)
-    ).reshape(2, T, 1, S * I)
-    readouts = jnp.stack([direct_readout, channel_readout]).reshape(2, H, HEAD_SIZE)
     wide = max(128, rpp * H)
     lanes = -(-C // 128) * 128
     bf, f32 = jnp.bfloat16, jnp.float32
@@ -289,6 +310,7 @@
         functools.partial(kernel, n, (T, S, I, J, H, G)),
         out_shape=jax.ShapeDtypeStruct((8, lanes), f32),
         in_specs=[
+            pl.BlockSpec(memory_space=smem),
             pl.BlockSpec(memory_space=smem),
             pl.BlockSpec(memory_space=smem),
             pl.BlockSpec(memory_space=vmem),
@@ -302,8 +324,9 @@
             vmem(target_queries.shape, bf),
             vmem((n, rpp, I, G * HEAD_SIZE), bf),
             vmem((n, rpp, I, G * HEAD_SIZE), bf),
-            vmem((n, I, wide), bf),
-            vmem((n, I, wide), bf),
+            vmem((n, I, wide), f32),
+            vmem((n, I, wide), f32),
+            vmem((3, T, 1, S * I), jnp.int32),
             vmem((G, T * J, hg * S * I), f32),
             vmem((hg * S * I, HEAD_SIZE), bf),
             vmem((rpp * G, wide, hg * J), bf),
@@ -317,7 +340,8 @@
             collective_id=0, has_side_effects=True, vmem_limit_bytes=60 << 20
         ),
     )(
-        table, target_length, spread, readouts,
+        candidate_row, candidate_length, target_length,
+        direct_readout.reshape(1, QW), channel_readout.reshape(1, QW),
         candidate_queries.reshape(T, S * I, QW),
         target_states, target_queries,
         candidate_states.reshape(n, rpp, I, 2 * G * HEAD_SIZE),

time: 49.2 us -> 46 us (0.935)
  other arithmetic: 2.78 us -> 0 us
  local copies, waits for them, and re-layouts: 4.29 us -> 3.79 us
    another operation x3 -> x0, other arithmetic: 2.03 us -> none  [the longest x1 1.31 us: on_device(): jnp.stack([direct_readout, channel_readout]).reshape(2, H, HEAD_SIZE)]
    reshape x1 -> x2, local copies, waits for them, and re-layouts: 0.69 us -> 2.61 us  [the longest x1 1.31 us: on_device(): channel_readout.reshape(1, QW)]
    another operation x2 -> x0, local copies, waits for them, and re-layouts: 0.85 us -> none  [on_device(): jnp.stack([jnp.arange(C, dtype=jnp.int32) // S, candidate_length.reshape(...]
    broadcast_in_dim x2 -> x0, local copies, waits for them, and re-layouts: 0.8 us -> none  [the longest x1 0.73 us: on_device(): jnp.broadcast_to(target_length[:, None], (T, S)).reshape(C)]
    eq x1 -> x0, local copies, waits for them, and re-layouts: 0.76 us -> none  [on_device(): matches = flat[None, :] == jnp.arange(C, dtype=jnp.int32)[:, None]]
    reduce_sum x1 -> x0, other arithmetic: 0.73 us -> none  [on_device(): table = jnp.sum(jnp.where(matches[None], each[:, None, :], 0), axis=2)]
where the time goes in v2:
time: 46 us; the launch traced here: 45.7 us
  Pallas kernels  41.9 us (91%)
  local copies, waits for them, and re-layouts  3.79 us (8%)
    pallas_call x1, Pallas kernels, on_device(): pl.pallas_call(functools.partial(kernel, n, (T, S, I, J, H, G)), out_shap...  41.9 us
    reshape x1, local copies, waits for them, and re-layouts, on_device(): channel_readout.reshape(1, QW)  1.31 us
    reshape x1, local copies, waits for them, and re-layouts, on_device(): direct_readout.reshape(1, QW)  1.3 us
    squeeze x1, local copies, waits for them, and re-layouts, on_device(): return found[0, :C]  1.18 us

profile of v2, /device:TPU:0, one launch (start us, length us, event | category | flops | bytes accessed | tf_op | source)
XLA Modules:
  0.0 45.7 jit_solution(147143595433961546)
XLA Ops:
  0.0 1.3 %reshape.12.direct_r = bf16[1,4096]{1,0:T(2,128)(2,1)} reshape(bf16[4096]{0:T(1024)(128)(2,1)} %param.16) | data formatting | bytes 16384 | tf_op jit(solution)/shard_map/reshape | solution.py:344
  1.3 1.3 %reshape.13.channel_r = bf16[1,4096]{1,0:T(2,128)(2,1)} reshape(bf16[4096]{0:T(1024)(128)(2,1)} %param.17) | data formatting | bytes 16384 | tf_op jit(solution)/shard_map/reshape | solution.py:344
  2.6 41.9 %shard_map.91 = f32[8,128]{1,0:T(8,128)} custom-call(s32[8,8]{1,0:T(8,128)} %stored.1, s32[8,8]{1,0:T(8,128)} %sources.1, s32[8]{0:T(128)} %lengths.1, bf16[1,4096]{1,0:T(2,128)(2,1)} %reshape.12.direct_r, bf16[1,4096]{1,0:T(2,128)(2,1)} %reshape.13.channel_r, bf16[8,128,4096]{2,1,0:T(8,128)(2,1)} %bitcast.4, bf16[8,32,1024]{2,1,0:T(8,128)(2,1)} %ts.1, ...), custom_call_target="tpu_custom_call" | custom-call | tf_op jit(solution)/shard_map/pallas_call | solution.py:309
  44.5 1.2 %slice_bitcast_fusion = f32[64]{0:T(128)} fusion(f32[8,128]{1,0:T(8,128)} %shard_map.91), kind=kLoop, calls=%fused_computation | loop fusion | bytes 512 | tf_op jit(solution)/shard_map/squeeze | solution.py:349

commit v3 on v2

--- a/solution.py
+++ b/solution.py
@@ -56,8 +56,9 @@
 
 def kernel(
     n, dims,
-    stored, sources, lengths, direct_r, channel_r, cq, ts, tq, cs,
+    stored_in, sources_in, lengths_in, direct_in, channel_in, cq, ts, tq, cs,
     out,
+    stored, sources, lengths, direct_r, channel_r,
     cq_buf, ts_buf, tq_buf, v_buf, k_buf, u_out, u_buf, spread, ud, rd, sel, dsum, r_out, r_buf,
     in_sem, cq_sem, ks, kr, us, ur, rs, rr,
 ):
@@ -75,10 +76,12 @@
         ),
         pltpu.make_async_copy(ts, ts_buf, in_sem.at[2]),
         pltpu.make_async_copy(tq, tq_buf, in_sem.at[3]),
+        pltpu.make_async_copy(channel_in, channel_r, in_sem.at[4]),
+        pltpu.make_async_copy(direct_in, direct_r, in_sem.at[5]),
+        pltpu.make_async_copy(stored_in, stored, in_sem.at[6]),
+        pltpu.make_async_copy(sources_in, sources, in_sem.at[7]),
+        pltpu.make_async_copy(lengths_in, lengths, in_sem.at[8]),
     ]
-    loads[0].start()
-    loads[2].start()
-
     def cq_copy(t):
         return pltpu.make_async_copy(cq.at[t], cq_buf.at[t], cq_sem.at[t])
 
@@ -91,6 +94,10 @@
         return carry
 
     lax.fori_loop(1, n, greet, 0)
+    for load in loads[4:]:
+        load.start()
+    loads[0].start()
+    loads[2].start()
     cq_copy(0).start()
 
     def k_copy(p, slot):
@@ -128,8 +135,9 @@
     wide = u_out.shape[2]
     head_id = lax.broadcasted_iota(jnp.int32, (H, D), 0)
     rows_r = jnp.zeros((H, D), jnp.float32)
+    loads[4].wait()
     for h in range(H):
-        row = channel_r[:, h * D : (h + 1) * D].astype(jnp.float32)
+        row = channel_r[h * D : (h + 1) * D].astype(jnp.float32).reshape(1, D)
         rows_r = jnp.where(head_id == h, row, rows_r)
     rows_r = jnp.concatenate([rows_r.astype(jnp.bfloat16)] * (wide // H), axis=0)
     row_id = lax.broadcasted_iota(jnp.int32, (wide, D), 0)
@@ -162,6 +170,8 @@
 
     rows = S * I
     slot = lax.broadcasted_iota(jnp.int32, (1, rows), 1) // I
+    for load in loads[5:]:
+        load.wait()
     for t in range(T):
         held = jnp.zeros((1, rows), jnp.int32)
         count = jnp.zeros((1, rows), jnp.int32)
@@ -178,7 +188,7 @@
         for q in range(hg):
             h = g * hg + q
             rd[q * rows : (q + 1) * rows, :] = jnp.broadcast_to(
-                direct_r[:, h * D : (h + 1) * D].astype(jnp.float32), (rows, D)
+                direct_r[h * D : (h + 1) * D].astype(jnp.float32).reshape(1, D), (rows, D)
             ).astype(jnp.bfloat16)
         ud[g] = dot_nt(states, rd[...])
 
@@ -310,15 +320,16 @@
         functools.partial(kernel, n, (T, S, I, J, H, G)),
         out_shape=jax.ShapeDtypeStruct((8, lanes), f32),
         in_specs=[
-            pl.BlockSpec(memory_space=smem),
-            pl.BlockSpec(memory_space=smem),
-            pl.BlockSpec(memory_space=smem),
-            pl.BlockSpec(memory_space=vmem),
-            pl.BlockSpec(memory_space=vmem),
+            anywhere, anywhere, anywhere, anywhere, anywhere,
             anywhere, anywhere, anywhere, anywhere,
         ],
         out_specs=pl.BlockSpec(memory_space=vmem),
         scratch_shapes=[
+            smem((T, S), jnp.int32),
+            smem((T, S), jnp.int32),
+            smem((T,), jnp.int32),
+            vmem((QW,), bf),
+            vmem((QW,), bf),
             vmem((T, S * I, QW), bf),
             vmem(target_states.shape, bf),
             vmem(target_queries.shape, bf),
@@ -333,7 +344,7 @@
             vmem((T, 1, S * I), f32),
             vmem((n, 8, lanes), f32),
             vmem((n, 8, lanes), f32),
-            dma((4,)), dma((T,)),
+            dma((9,)), dma((T,)),
             dma((n,)), dma((n,)), dma((n,)), dma((n,)), dma((n,)), dma((n,)),
         ],
         compiler_params=pltpu.CompilerParams(
@@ -341,7 +352,7 @@
         ),
     )(
         candidate_row, candidate_length, target_length,
-        direct_readout.reshape(1, QW), channel_readout.reshape(1, QW),
+        direct_readout, channel_readout,
         candidate_queries.reshape(T, S * I, QW),
         target_states, target_queries,
         candidate_states.reshape(n, rpp, I, 2 * G * HEAD_SIZE),

time: 46 us -> 42.2 us (0.917)
  local copies, waits for them, and re-layouts: 3.79 us -> 1.19 us
  Pallas kernels: 41.9 us -> 40.8 us
    reshape x2 -> x0, local copies, waits for them, and re-layouts: 2.61 us -> none  [the longest x1 1.31 us: on_device(): channel_readout.reshape(1, QW)]
    pallas_call x1, Pallas kernels: 41.9 us -> 40.8 us  [on_device(): pl.pallas_call(functools.partial(kernel, n, (T, S, I, J, H, G)), out_shap...]
where the time goes in v3:
time: 42.2 us; the launch traced here: 42 us
  Pallas kernels  40.8 us (97%)
  local copies, waits for them, and re-layouts  1.19 us (3%)
    pallas_call x1, Pallas kernels, on_device(): pl.pallas_call(functools.partial(kernel, n, (T, S, I, J, H, G)), out_shap...  40.8 us
    squeeze x1, local copies, waits for them, and re-layouts, on_device(): return found[0, :C]  1.19 us

profile of v3, /device:TPU:0, one launch (start us, length us, event | category | flops | bytes accessed | tf_op | source)
XLA Modules:
  0.0 42.0 jit_solution(17681010426823943460)
XLA Ops:
  0.0 40.8 %shard_map.91 = f32[8,128]{1,0:T(8,128)} custom-call(s32[8,8]{1,0:T(8,128)} %stored_in.1, s32[8,8]{1,0:T(8,128)} %sources_in.1, s32[8]{0:T(128)} %lengths_in.1, bf16[4096]{0:T(1024)(128)(2,1)} %direct_in.1, bf16[4096]{0:T(1024)(128)(2,1)} %channel_in.1, bf16[8,128,4096]{2,1,0:T(8,128)(2,1)} %bitcast.4, bf16[8,32,1024]{2,1,0:T(8,128)(2,1)} %ts.1, ...), custom_call_target="tpu_custom_call" | custom-call | tf_op jit(solution)/shard_map/pallas_call | solution.py:319
  40.8 1.2 %slice_bitcast_fusion = f32[64]{0:T(128)} fusion(f32[8,128]{1,0:T(8,128)} %shard_map.91), kind=kLoop, calls=%fused_computation | loop fusion | bytes 512 | tf_op jit(solution)/shard_map/squeeze | solution.py:360
